TPU v7x, 1024 devices: a whole 4x8x16 slice. The times are simulated.
1024 devices in a mesh: row: 16 (over y, core), col: 32 (over x, z_lo), layer: 2 (over z_hi).
Axes of the slice: x: 4, y: 8, z: 16 (z_hi: 2, z_lo: 8; z = z_hi * 8 + z_lo), core: 2. Of those that a mesh axis runs over, the one named last changes fastest.
Arguments:
- density: float32 [16, 32, 128, 9, 128], P('row', 'col'), as said below
- retained: int32 [16, 32, 2, 9, 2], P('row', 'col'), may hold values from 0 to 1, as said below
Outputs:
- purified: float32 [16, 32, 128, 9, 128], P('row', 'col', None, None, 'layer')
Inputs may be any that keep to these rules, and one draw needn't show every extreme that they name: retained is 1 for the block of every atom with itself (offset index 4, equal atoms). density is zero wherever retained is 0.
All inputs are finite; a program needn't handle non-finite values.
Results may differ from a plain program's by a relative error of at most 0.00014.
Values sent between devices are 32-bit elements; how exact they have to be, the bound alone decides.
A program may use at most 32 MiB of HBM per device.

v0:
```python
import jax
import jax.numpy as jnp
from jax import lax
from jax.sharding import PartitionSpec as P


def from_behind(block, axis, distance):
    devices = range(lax.axis_size(axis))
    route = [((i - distance) % len(devices), i) for i in devices]
    return lax.ppermute(block, axis, route)


def shift_rows(payload, amount):
    return from_behind(payload, "row", amount)


def shift_cols(payload, amount):
    return from_behind(payload, "col", amount)


def neighbour_blocks(source):
    row_count = source.shape[0]
    col_count = source.shape[2]
    lattice = source.reshape(row_count, 3, 3, col_count)
    blocks = {(0, 0): lattice}
    for step_x in (-1, 1):
        start_at = max(0, -step_x)
        blocks[step_x, 0] = shift_rows(lattice[:, start_at : start_at + 2], -step_x)
    for step_y in (-1, 1):
        start_at = max(0, -step_y)
        bundle = jnp.concatenate(
            [
                blocks[-1, 0][:, :, start_at : start_at + 2],
                lattice[:, :, start_at : start_at + 2],
                blocks[1, 0][:, :, start_at : start_at + 2],
            ],
            axis=1,
        )
        arrived = shift_cols(bundle, -step_y)
        blocks[-1, step_y] = arrived[:, 0:2]
        blocks[0, step_y] = arrived[:, 2:5]
        blocks[1, step_y] = arrived[:, 5:7]
    return blocks


def block_product(factor, blocks):
    height = factor.shape[0]
    inner_rows = factor.shape[2]
    breadth = blocks[0, 0].shape[3]
    accumulated = jnp.zeros((height, 3, 3, breadth), jnp.float32)
    for step_x in (-1, 0, 1):
        for step_y in (-1, 0, 1):
            neighbour = blocks[step_x, step_y]
            span_x = neighbour.shape[1]
            span_y = neighbour.shape[2]
            product_term = jnp.dot(
                factor[:, 3 * (step_x + 1) + (step_y + 1), :],
                neighbour.reshape(inner_rows, span_x * span_y * breadth),
                precision=lax.Precision.HIGHEST,
                preferred_element_type=jnp.float32,
            )
            start_x = max(step_x, 0)
            start_y = max(step_y, 0)
            accumulated = accumulated.at[
                :, start_x : start_x + span_x, start_y : start_y + span_y, :
            ].add(product_term.reshape(height, span_x, span_y, breadth))
    return accumulated.reshape(height, 9, breadth)


def body(density, retained):
    matrix = density[0, 0]
    pattern = retained[0, 0]
    full_width = matrix.shape[0]
    atom_count = pattern.shape[0]
    block_size = full_width // atom_count
    keeper = jnp.broadcast_to(
        pattern.astype(jnp.float32)[:, None, :, :, None],
        (atom_count, block_size, 9, atom_count, block_size),
    ).reshape(full_width, 9, full_width)
    portion = full_width // lax.axis_size("layer")
    layer_start = lax.axis_index("layer") * portion
    keep_half = lax.dynamic_slice_in_dim(keeper, layer_start, portion, 2)
    source = lax.dynamic_slice_in_dim(matrix, layer_start, portion, 2)
    blocks = neighbour_blocks(source)
    square_half = block_product(matrix, blocks) * keep_half
    cube_half = (
        block_product(lax.all_gather(square_half, "layer", axis=2, tiled=True), blocks) * keep_half
    )
    purified = 3.0 * square_half - 2.0 * cube_half
    return purified[None, None]


def solution(mesh):
    placed = (P("row", "col", None, None, None), P("row", "col", None, None, None))
    return jax.shard_map(
        body,
        mesh=mesh,
        in_specs=placed,
        out_specs=P("row", "col", None, None, "layer"),
        check_vma=False,
    )
```

profile of v0, /device:TPU:196, one launch (start us, length us, event | category | flops | bytes accessed | tf_op | source)
XLA Modules:
  0.0 86.0 jit_solution(673362392185024414)
XLA Ops:
  0.0 1.3 %constant_dynamic-slice_fusion = f32[1,1,128,9,64]{4,2,3,1,0:T(8,128)S(1)} fusion(f32[1,1,128,9,128]{4,2,3,1,0:T(8,128)} %param.42, s32[]{:T(128)S(6)} %select_n.4), kind=kLoop, calls=%fused_computation.71 | loop fusion | bytes 589828 | tf_op jit(solution)/shard_map/dynamic_slice | solution.py:83
  1.6 2.9 %collective-permute-start.1 = (f32[128,2,3,64]{0,3,2,1:T(8,128)S(1)}, f32[128,2,3,64]{0,3,2,1:T(8,128)S(1)}, u32[]{:S(2)}, u32[]{:S(2)}) collective-permute-start(f32[128,2,3,64]{0,3,2,1:T(8,128)S(1)} %get-tuple-element.246), channel_id=1, source_target_pairs={{64,0},{128,64},{192,128},{256,192},{320,256},{384,320},{448,384},... | collective-permute-start | bytes 589832 | tf_op jit(solution)/shard_map/ppermute | solution.py:10
  4.5 0.6 fusion.50
  5.2 0.4 broadcast_in_dim.4
  5.6 0.6 reshape.769
  6.3 0.4 copy-done
  6.7 0.4 fusion.33
  7.1 0.6 collective-permute-done.1
  7.9 5.5 %collective-permute-start.2 = (f32[128,7,2,64]{0,3,2,1:T(8,128)S(1)}, f32[128,7,2,64]{0,3,2,1:T(8,128)S(1)}, u32[]{:S(2)}, u32[]{:S(2)}) collective-permute-start(f32[128,7,2,64]{0,3,2,1:T(8,128)S(1)} %pad_maximum_fusion), channel_id=1, source_target_pairs={{62,0},{0,2},{2,4},{4,6},{6,8},{8,10},{10,12},{12,14},{14,16},{16,... | collective-permute-start | bytes 1376264 | tf_op jit(solution)/shard_map/ppermute | solution.py:10
  13.5 1.9 %collective-permute-start.3 = (f32[128,7,2,64]{0,3,2,1:T(8,128)S(1)}, f32[128,7,2,64]{0,3,2,1:T(8,128)S(1)}, u32[]{:S(2)}, u32[]{:S(2)}) collective-permute-start(f32[128,7,2,64]{0,3,2,1:T(8,128)S(1)} %pad_maximum_fusion.1), channel_id=1, source_target_pairs={{2,0},{4,2},{6,4},{8,6},{10,8},{12,10},{14,12},{16,14},{18,16},{20... | collective-permute-start | bytes 1376264 | tf_op jit(solution)/shard_map/ppermute | solution.py:10
  15.4 0.3 fusion.36
  15.7 0.3 fusion.30
  16.1 7.8 %collective-permute-done.2 = f32[128,7,2,64]{0,3,2,1:T(8,128)S(1)} collective-permute-done((f32[128,7,2,64]{0,3,2,1:T(8,128)S(1)}, f32[128,7,2,64]{0,3,2,1:T(8,128)S(1)}, u32[]{:S(2)}, u32[]{:S(2)}) %collective-permute-start.2) | collective-permute-done | bytes 458784 | tf_op jit(solution)/shard_map/ppermute | solution.py:10
  24.5 0.3 fusion.34
  24.8 14.3 %collective-permute-done.3 = f32[128,7,2,64]{0,3,2,1:T(8,128)S(1)} collective-permute-done((f32[128,7,2,64]{0,3,2,1:T(8,128)S(1)}, f32[128,7,2,64]{0,3,2,1:T(8,128)S(1)}, u32[]{:S(2)}, u32[]{:S(2)}) %collective-permute-start.3) | collective-permute-done | bytes 458784 | tf_op jit(solution)/shard_map/ppermute | solution.py:10
  39.1 0.3 fusion.32
  40.1 1.2 %add_dynamic-update-slice_fusion.2 = f32[128,3,3,64]{0,3,2,1:T(8,128)S(1)} fusion(f32[128,3,3,64]{0,3,2,1:T(8,128)S(1)} %add_dynamic-update-slice_fusion.1, s32[]{:T(128)} %bitcast.10, s32[]{:T(128)} %bitcast.11, f32[128,2,2,64]{0,3,2,1:T(8,128)S(1)} %bitcast.246), kind=kLoop, calls=%fused_computation.41 | loop fusion | flops 32768 | bytes 393224 | tf_op jit(solution)/shard_map/scatter-add | solution.py:66
  41.7 39.3 %all_gather.3 = f32[128,9,128]{0,2,1:T(8,128)S(1)} all-gather(f32[128,9,64]{0,2,1:T(8,128)S(1)} %bitcast_multiply_fusion.1), channel_id=1, replica_groups=mesh['row'=16,'col'=32,'layer'=2] {'layer'}, dimensions={2}, use_global_device_ids=true | all-gather | bytes 884736 | tf_op jit(solution)/shard_map/all_gather | solution.py:87
  81.3 0.4 add_dynamic-update-slice_fusion
  81.7 1.5 %fusion.2 = f32[128,3,3,64]{0,3,2,1:T(8,128)S(1)} fusion(f32[128,3,3,64]{0,3,2,1:T(8,128)S(1)} %add_dynamic-update-slice_fusion, s32[]{:T(128)} %bitcast.10, s32[]{:T(128)} %bitcast.11, f32[128,9,128]{0,2,1:T(8,128)S(1)} %all_gather.3, f32[128,7,2,64]{0,3,2,1:T(8,128)S(1)} %collective-permute-done.3), kind=kOutput, calls=%fused_computation.7 | convolution fusion | flops 50364416 | bytes 458760 | tf_op jit(solution)/shard_map/dot_general | solution.py:56
  83.2 0.4 fusion.1
  83.5 0.4 convolution_add_fusion
  83.9 0.4 fusion
  85.2 0.8 fusion.4
  (38 shorter events, 3.4 us)
Async XLA Ops:
  0.0 5.1 %copy-start.1 = (s32[1,1,2,9,2]{3,4,2,1,0:T(2,128)S(1)}, s32[1,1,2,9,2]{3,4,2,1,0:T(2,128)}, u32[]{:S(2)}) copy-start(s32[1,1,2,9,2]{3,4,2,1,0:T(2,128)} %param.43) | copy-start | bytes 436
  1.6 6.3 %collective-permute-start = (f32[128,2,3,64]{0,3,2,1:T(8,128)S(1)}, f32[128,2,3,64]{0,3,2,1:T(8,128)S(1)}, u32[]{:S(2)}, u32[]{:S(2)}) collective-permute-start(f32[128,2,3,64]{0,3,2,1:T(8,128)S(1)} %get-tuple-element.245), channel_id=1, source_target_pairs={{960,0},{0,64},{64,128},{128,192},{192,256},{256,320},{320,384},{3... | collective-permute-start | bytes 589832 | tf_op jit(solution)/shard_map/ppermute | solution.py:10
  1.6 6.1 %collective-permute-start.1 = (f32[128,2,3,64]{0,3,2,1:T(8,128)S(1)}, f32[128,2,3,64]{0,3,2,1:T(8,128)S(1)}, u32[]{:S(2)}, u32[]{:S(2)}) collective-permute-start(f32[128,2,3,64]{0,3,2,1:T(8,128)S(1)} %get-tuple-element.246), channel_id=1, source_target_pairs={{64,0},{128,64},{192,128},{256,192},{320,256},{384,320},{448,384},... | collective-permute-start | bytes 589832 | tf_op jit(solution)/shard_map/ppermute | solution.py:10
  5.6 1.1 %copy-start = (f32[1,1,128,9,128]{4,2,3,1,0:T(8,128)S(1)}, f32[1,1,128,9,128]{4,2,3,1,0:T(8,128)}, u32[]{:S(2)}) copy-start(f32[1,1,128,9,128]{4,2,3,1,0:T(8,128)} %param.42) | copy-start | bytes 1769476
  7.9 15.9 %collective-permute-start.2 = (f32[128,7,2,64]{0,3,2,1:T(8,128)S(1)}, f32[128,7,2,64]{0,3,2,1:T(8,128)S(1)}, u32[]{:S(2)}, u32[]{:S(2)}) collective-permute-start(f32[128,7,2,64]{0,3,2,1:T(8,128)S(1)} %pad_maximum_fusion), channel_id=1, source_target_pairs={{62,0},{0,2},{2,4},{4,6},{6,8},{8,10},{10,12},{12,14},{14,16},{16,... | collective-permute-start | bytes 1376264 | tf_op jit(solution)/shard_map/ppermute | solution.py:10
  13.5 25.6 %collective-permute-start.3 = (f32[128,7,2,64]{0,3,2,1:T(8,128)S(1)}, f32[128,7,2,64]{0,3,2,1:T(8,128)S(1)}, u32[]{:S(2)}, u32[]{:S(2)}) collective-permute-start(f32[128,7,2,64]{0,3,2,1:T(8,128)S(1)} %pad_maximum_fusion.1), channel_id=1, source_target_pairs={{2,0},{4,2},{6,4},{8,6},{10,8},{12,10},{14,12},{16,14},{18,16},{20... | collective-permute-start | bytes 1376264 | tf_op jit(solution)/shard_map/ppermute | solution.py:10
where the time goes:
time: 86.3 us; the launch traced here: 86 us
  blocking collectives  39.3 us (46%)
  waiting for transfers between devices  22.8 us (26%)
  starting transfers between devices  10.4 us (12%)
  matrix products  6.92 us (8%)
  local copies, waits for them, and re-layouts  3.85 us (4%)
  other arithmetic  2.45 us (3%)
    all_gather x1, blocking collectives, body(): lax.all_gather(square_half, 'layer', axis=2, tiled=True)  39.3 us
    ppermute x4, waiting for transfers between devices, from_behind(): return lax.ppermute(block, axis, route)  22.8 us
    ppermute x4, starting transfers between devices, from_behind(): return lax.ppermute(block, axis, route)  10.4 us
    dot_general x18, matrix products, block_product(): jnp.dot(factor[:, 3 * (step_x + 1) + (step_y + 1), :], neighbour.reshape(...  6.92 us
  transfers between devices with their start and end apart: 4, of which 4 were waited for; matrix products, arithmetic and copies ran while one was open for 4% of the time, Pallas kernels for 0%

commit v1 on v0

v1 whole, which is shorter than its diff:
```python
import jax
import jax.numpy as jnp
from jax import lax
from jax.experimental import pallas as pl
from jax.experimental.pallas import tpu as pltpu
from jax.sharding import PartitionSpec as P

MESH = pl.DeviceIdType.MESH
RUN = 8


def reach(step):
    return max(0, 1 - step), 3 - abs(step - 1)


def split(value):
    high = value.astype(jnp.bfloat16)
    low = (value - high.astype(jnp.float32)).astype(jnp.bfloat16)
    return high, low


def kernel(rows, cols, run, p_hbm, kept, out_ref, got, high, low, left, square, cube,
           local_sem, send_z, recv_z, send_row, recv_row, send_fwd, recv_fwd):
    row, col, layer = lax.axis_index("row"), lax.axis_index("col"), lax.axis_index("layer")
    parity = lax.rem(row, 2)
    far, near = 2 * parity, 2 - 2 * parity
    far_dev = (lax.rem(row + far - 1 + rows, rows), col, layer)
    near_dev = (lax.rem(row + near - 1 + rows, rows), col, layer)
    place = lax.rem(col, run)
    after = (row, lax.rem(col + 1, cols), lax.rem(layer + lax.div(place + 1, run), 2))
    before = (row, lax.rem(col + cols - 1, cols), lax.rem(layer + lax.div(run - place, run), 2))

    barrier = pltpu.get_barrier_semaphore()
    for device in (after, before, far_dev, near_dev):
        pl.semaphore_signal(barrier, inc=1, device_id=device, device_id_type=MESH)
    own = pltpu.make_async_copy(p_hbm, got.at[1, 1], local_sem)
    own.start()
    pl.semaphore_wait(barrier, 4)

    def remote(src, dst, sems, rsems, place, device):
        return pltpu.make_async_remote_copy(
            src_ref=src, dst_ref=dst, send_sem=sems.at[place], recv_sem=rsems.at[place],
            device_id=device, device_id_type=MESH)

    sides = ((before, 2, 0), (after, 0, 1))
    z_copies = {}
    for part, which in enumerate((1, far, near)):
        for side, (device, step, start) in enumerate(sides):
            z_copies[part, side] = remote(
                p_hbm.at[which, pl.ds(start, 2)], got.at[1, step, which, pl.ds(start, 2)],
                send_z, recv_z, (part, side), device)
    row_copies = [
        remote(p_hbm.at[pl.ds(parity, 2)], got.at[near, 1, pl.ds(parity, 2)],
               send_row, recv_row, 0, far_dev),
        remote(p_hbm.at[pl.ds(1 - parity, 2)], got.at[far, 1, pl.ds(1 - parity, 2)],
               send_row, recv_row, 1, near_dev),
    ]
    z_copies[0, 0].start()
    z_copies[0, 1].start()
    row_copies[0].start()
    row_copies[1].start()
    for part in (1, 2):
        for side in (0, 1):
            z_copies[part, side].start()

    def forward(slot, which, side, device, place):
        step, start = sides[side][1:]
        return remote(got.at[1, step, which, pl.ds(start, 2)],
                      got.at[place, step, which, pl.ds(start, 2)],
                      send_fwd, recv_fwd, (slot, side), device)

    def load(step_x, step_y):
        first_x, count_x = reach(step_x)
        first_y, count_y = reach(step_y)
        for rx in range(first_x, first_x + count_x):
            for ry in range(first_y, first_y + count_y):
                h, l = split(got[step_x, step_y, rx, ry])
                high[step_x, step_y, rx, :, 128 * ry : 128 * ry + 128] = h
                low[step_x, step_y, rx, :, 128 * ry : 128 * ry + 128] = l

    def multiply(total, step_x, step_y):
        first_x, count_x = reach(step_x)
        first_y, count_y = reach(step_y)
        factor = left[3 * step_x + step_y]
        lanes = pl.ds(128 * first_y, 128 * count_y)
        target = pl.ds(128 * (first_y + step_y - 1), 128 * count_y)
        for rx in range(first_x, first_x + count_x):
            both = jnp.dot(factor, high[step_x, step_y, rx, :, lanes],
                           preferred_element_type=jnp.float32)
            rest = jnp.dot(factor[:128], low[step_x, step_y, rx, :, lanes],
                           preferred_element_type=jnp.float32)
            total[rx + step_x - 1, :, target] += both[:128] + (both[128:] + rest)

    square[...] = jnp.zeros_like(square)
    cube[...] = jnp.zeros_like(cube)
    own.wait()
    load(1, 1)
    for index in range(9):
        left[index, :128] = high[1, 1, index // 3, :, 128 * (index % 3) : 128 * (index % 3) + 128]
        left[index, 128:] = low[1, 1, index // 3, :, 128 * (index % 3) : 128 * (index % 3) + 128]
    multiply(square, 1, 1)

    forwards = []

    def send_on(slot, which, side, device, place):
        copy = forward(slot, which, side, device, place)
        copy.start()
        forwards.append(copy)

    for side in (0, 1):
        z_copies[0, side].wait_recv()
        send_on(0, 1, side, far_dev, near)
        send_on(1, 1, side, near_dev, far)
    row_copies[1].wait_recv()
    row_copies[0].wait_recv()
    for step_x in (0, 2):
        load(step_x, 1)
        multiply(square, step_x, 1)
    for side in (0, 1):
        z_copies[1, side].wait_recv()
        send_on(2, far, side, far_dev, near)
    for side in (0, 1):
        z_copies[2, side].wait_recv()
        send_on(3, near, side, near_dev, far)
    for step_y in (0, 2):
        load(1, step_y)
        multiply(square, 1, step_y)
    for copy in forwards:
        copy.wait_recv()
    for step_x in (0, 2):
        for step_y in (0, 2):
            load(step_x, step_y)
            multiply(square, step_x, step_y)

    upper = lax.broadcasted_iota(jnp.int32, (128, 128), 0) < 64
    first = lax.broadcasted_iota(jnp.int32, (128, 128), 1) < 64

    def keep(index):
        scale = [[kept[a, b, index].astype(jnp.float32) for b in range(2)] for a in range(2)]
        return jnp.where(upper, jnp.where(first, scale[0][0], scale[0][1]),
                         jnp.where(first, scale[1][0], scale[1][1]))

    for index in range(9):
        lanes = pl.ds(128 * (index % 3), 128)
        value = square[index // 3, :, lanes] * keep(index)
        square[index // 3, :, lanes] = value
        h, l = split(value)
        left[index, :128] = h
        left[index, 128:] = l
    for index in range(9):
        multiply(cube, index // 3, index % 3)
    for index in range(9):
        lanes = pl.ds(128 * (index % 3), 128)
        value = 3.0 * square[index // 3, :, lanes] - 2.0 * (cube[index // 3, :, lanes] * keep(index))
        out_ref[index] = jnp.where(layer == 0, value[:, :64], value[:, 64:])

    for copy in list(z_copies.values()) + row_copies + forwards:
        copy.wait_send()


def solution(mesh):
    sizes = dict(mesh.shape)
    rows, cols = sizes["row"], sizes["col"]
    run = min(RUN, cols)

    def whole(*args):
        kernel(rows, cols, run, *args)

    def body(density, retained):
        blocks = density[0, 0].transpose(1, 0, 2).reshape(3, 3, 128, 128)
        kept = retained[0, 0].transpose(0, 2, 1)
        f32, bf16 = jnp.float32, jnp.bfloat16
        dma = pltpu.SemaphoreType.DMA
        result = pl.pallas_call(
            whole,
            out_shape=jax.ShapeDtypeStruct((9, 128, 64), f32),
            in_specs=[pl.BlockSpec(memory_space=pl.ANY), pl.BlockSpec(memory_space=pltpu.SMEM)],
            out_specs=pl.BlockSpec(memory_space=pltpu.VMEM),
            scratch_shapes=[
                pltpu.VMEM((3, 3, 3, 3, 128, 128), f32),
                pltpu.VMEM((3, 3, 3, 128, 384), bf16),
                pltpu.VMEM((3, 3, 3, 128, 384), bf16),
                pltpu.VMEM((9, 256, 128), bf16),
                pltpu.VMEM((3, 128, 384), f32),
                pltpu.VMEM((3, 128, 384), f32),
                dma, dma((3, 2)), dma((3, 2)), dma((2,)), dma((2,)), dma((4, 2)), dma((4, 2)),
            ],
            compiler_params=pltpu.CompilerParams(
                collective_id=0, has_side_effects=True, vmem_limit_bytes=40 << 20),
        )(blocks, kept)
        return result.transpose(1, 0, 2)[None, None]

    placed = P("row", "col", None, None, None)
    return jax.shard_map(body, mesh=mesh, in_specs=(placed, placed),
                         out_specs=P("row", "col", None, None, "layer"), check_vma=False)
```

time: 86.3 us -> 39.1 us (0.45)
  the two profiles are of different devices: /device:TPU:196 before, /device:TPU:1 now
where the time goes in v1:
time: 39.1 us; the launch traced here: 38.9 us
  Pallas kernels  36.2 us (93%)
  local copies, waits for them, and re-layouts  2.68 us (7%)
    pallas_call x1, Pallas kernels, body(): pl.pallas_call(whole, out_shape=jax.ShapeDtypeStruct((9, 128, 64), f32),...  36.2 us
    unnamed x4, local copies, waits for them, and re-layouts  1.74 us
    broadcast_in_dim x1, local copies, waits for them, and re-layouts, body(): return result.transpose(1, 0, 2)[None, None]  0.93 us

profile of v1, /device:TPU:1, one launch (start us, length us, event | category | flops | bytes accessed | tf_op | source)
XLA Modules:
  0.0 38.9 jit_solution(3729932440619800233)
XLA Ops:
  0.0 0.0 copy-start.1
  0.0 0.7 %copy-done.1 = s32[1,1,2,9,2]{3,4,2,1,0:T(2,128)S(1)} copy-done((s32[1,1,2,9,2]{3,4,2,1,0:T(2,128)S(1)}, s32[1,1,2,9,2]{3,4,2,1,0:T(2,128)}, u32[]{:S(2)}) %copy-start.1) | copy-done | bytes 168
  0.7 0.0 copy-start
  0.7 1.1 %copy-done = f32[1,1,128,9,128]{4,2,3,1,0:T(8,128)S(1)} copy-done((f32[1,1,128,9,128]{4,2,3,1,0:T(8,128)S(1)}, f32[1,1,128,9,128]{4,2,3,1,0:T(8,128)}, u32[]{:S(2)}) %copy-start) | copy-done | bytes 589848
  1.7 36.2 %shard_map.28 = f32[9,128,64]{2,1,0:T(8,128)S(1)} custom-call(f32[3,3,128,128]{3,2,1,0:T(8,128)S(1)} %bitcast.12, s32[2,2,9]{2,1,0:T(2,128)S(1)} %bitcast.13), custom_call_target="tpu_custom_call" | custom-call | tf_op jit(solution)/shard_map/pallas_call | solution.py:174
  37.9 0.9 %copy.3 = f32[1,1,128,9,64]{2,4,3,1,0:T(8,128)} copy(f32[1,1,128,9,64]{4,2,3,1,0:T(8,128)S(1)} %bitcast.11) | data formatting | bytes 589824 | tf_op jit(solution)/shard_map/broadcast_in_dim | solution.py:191
Async XLA Ops:
  0.0 0.7 %copy-start.1 = (s32[1,1,2,9,2]{3,4,2,1,0:T(2,128)S(1)}, s32[1,1,2,9,2]{3,4,2,1,0:T(2,128)}, u32[]{:S(2)}) copy-start(s32[1,1,2,9,2]{3,4,2,1,0:T(2,128)} %param.3) | copy-start | bytes 436
  0.7 1.1 %copy-start = (f32[1,1,128,9,128]{4,2,3,1,0:T(8,128)S(1)}, f32[1,1,128,9,128]{4,2,3,1,0:T(8,128)}, u32[]{:S(2)}) copy-start(f32[1,1,128,9,128]{4,2,3,1,0:T(8,128)} %param.2) | copy-start | bytes 1769476

commit v2 on v1

v2 whole, which is shorter than its diff:
```python
import jax
import jax.numpy as jnp
from jax import lax
from jax.experimental import pallas as pl
from jax.experimental.pallas import tpu as pltpu
from jax.sharding import PartitionSpec as P

MESH = pl.DeviceIdType.MESH
RUN = 8


def reach(step):
    return max(0, 1 - step), 3 - abs(step - 1)


def split(value):
    high = value.astype(jnp.bfloat16)
    low = (value - high.astype(jnp.float32)).astype(jnp.bfloat16)
    return high, low


def kernel(rows, cols, run, p_hbm, kept_hbm, out_ref, kept, got, high, low, left, left_cube, square,
           cube, local_sem, kept_sem, send_z, recv_z, send_row, recv_row, send_fwd, recv_fwd):
    row, col, layer = lax.axis_index("row"), lax.axis_index("col"), lax.axis_index("layer")
    parity = lax.rem(row, 2)
    far, near = 2 * parity, 2 - 2 * parity
    far_dev = (lax.rem(row + far - 1 + rows, rows), col, layer)
    near_dev = (lax.rem(row + near - 1 + rows, rows), col, layer)
    place = lax.rem(col, run)
    after = (row, lax.rem(col + 1, cols), lax.rem(layer + lax.div(place + 1, run), 2))
    before = (row, lax.rem(col + cols - 1, cols), lax.rem(layer + lax.div(run - place, run), 2))

    barrier = pltpu.get_barrier_semaphore()
    for device in (after, before, far_dev, near_dev):
        pl.semaphore_signal(barrier, inc=1, device_id=device, device_id_type=MESH)
    own = pltpu.make_async_copy(p_hbm, got.at[1, 1], local_sem)
    own.start()
    pattern = pltpu.make_async_copy(kept_hbm, kept, kept_sem)
    pattern.start()
    pl.semaphore_wait(barrier, 4)

    def remote(src, dst, sems, rsems, place, device):
        return pltpu.make_async_remote_copy(
            src_ref=src, dst_ref=dst, send_sem=sems.at[place], recv_sem=rsems.at[place],
            device_id=device, device_id_type=MESH)

    sides = ((before, 2, 0), (after, 0, 1))
    z_copies = {}
    for part, which in enumerate((1, far, near)):
        for side, (device, step, start) in enumerate(sides):
            z_copies[part, side] = remote(
                p_hbm.at[which, pl.ds(start, 2)], got.at[1, step, which, pl.ds(start, 2)],
                send_z, recv_z, (part, side), device)
    row_copies = [
        remote(p_hbm.at[pl.ds(parity, 2)], got.at[near, 1, pl.ds(parity, 2)],
               send_row, recv_row, 0, far_dev),
        remote(p_hbm.at[pl.ds(1 - parity, 2)], got.at[far, 1, pl.ds(1 - parity, 2)],
               send_row, recv_row, 1, near_dev),
    ]
    z_copies[0, 0].start()
    z_copies[0, 1].start()
    row_copies[0].start()
    row_copies[1].start()
    for part in (1, 2):
        for side in (0, 1):
            z_copies[part, side].start()

    def forward(slot, which, side, device, place):
        step, start = sides[side][1:]
        return remote(got.at[1, step, which, pl.ds(start, 2)],
                      got.at[place, step, which, pl.ds(start, 2)],
                      send_fwd, recv_fwd, (slot, side), device)

    def load(step_x, step_y, rx):
        first, count = reach(step_y)
        for ry in range(first, first + count):
            h, l = split(got[step_x, step_y, rx, ry])
            high[step_x, step_y, rx, :, 128 * ry : 128 * ry + 128] = h
            low[step_x, step_y, rx, :, 128 * ry : 128 * ry + 128] = l

    def multiply(total, factors, step_x, step_y, rx):
        first, count = reach(step_y)
        factor = factors[step_x, step_y]
        lanes = pl.ds(128 * first, 128 * count)
        target = pl.ds(128 * (first + step_y - 1), 128 * count)
        both = jnp.dot(factor, high[step_x, step_y, rx, :, lanes],
                       preferred_element_type=jnp.float32)
        rest = jnp.dot(factor[:128], low[step_x, step_y, rx, :, lanes],
                       preferred_element_type=jnp.float32)
        total[rx + step_x - 1, :, target] += both[:128] + (both[128:] + rest)

    def add_square(step_x, step_y, rx):
        load(step_x, step_y, rx)
        multiply(square, left, step_x, step_y, rx)

    def add_cube(step_x, step_y, rx):
        multiply(cube, left_cube, step_x, step_y, rx)

    upper = lax.broadcasted_iota(jnp.int32, (128, 128), 0) < 64
    first_half = lax.broadcasted_iota(jnp.int32, (128, 128), 1) < 64

    def keep(index):
        scale = [[kept[a, b, index].astype(jnp.float32) for b in range(2)] for a in range(2)]
        return jnp.where(upper, jnp.where(first_half, scale[0][0], scale[0][1]),
                         jnp.where(first_half, scale[1][0], scale[1][1]))

    def finish_square(target_x):
        for target_y in range(3):
            lanes = pl.ds(128 * target_y, 128)
            value = square[target_x, :, lanes] * keep(3 * target_x + target_y)
            square[target_x, :, lanes] = value
            h, l = split(value)
            left_cube[target_x, target_y, :128] = h
            left_cube[target_x, target_y, 128:] = l

    square[...] = jnp.zeros_like(square)
    cube[...] = jnp.zeros_like(cube)
    own.wait()
    pattern.wait()
    for rx in range(3):
        load(1, 1, rx)
        for ry in range(3):
            lanes = pl.ds(128 * ry, 128)
            left[rx, ry, :128] = high[1, 1, rx, :, lanes]
            left[rx, ry, 128:] = low[1, 1, rx, :, lanes]
    for rx in range(3):
        multiply(square, left, 1, 1, rx)
    row_copies[1].wait_recv()
    add_square(near, 1, 1)
    add_square(near, 1, far)

    forwards = {}

    def send_on(slot, which, side, device, place):
        copy = forward(slot, which, side, device, place)
        copy.start()
        forwards[slot, side] = copy

    for side in (0, 1):
        z_copies[0, side].wait_recv()
        send_on(0, 1, side, far_dev, near)
        send_on(1, 1, side, near_dev, far)
    for step_y in (2, 0):
        add_square(1, step_y, 1)
    row_copies[0].wait_recv()
    add_square(far, 1, 1)
    add_square(far, 1, near)
    for side in (0, 1):
        z_copies[1, side].wait_recv()
        send_on(2, far, side, far_dev, near)
    for step_y in (2, 0):
        add_square(1, step_y, far)
    for side in (0, 1):
        forwards[1, side].wait_recv()
    for step_y in (2, 0):
        add_square(near, step_y, 1)
    for side in (0, 1):
        z_copies[2, side].wait_recv()
        send_on(3, near, side, near_dev, far)
    for step_y in (2, 0):
        add_square(1, step_y, near)
    finish_square(near)
    for step_y in range(3):
        if step_y == 1:
            add_cube(near, 1, far)
        add_cube(near, step_y, 1)
    for side in (0, 1):
        forwards[0, side].wait_recv()
    for step_y in (2, 0):
        add_square(far, step_y, 1)
    finish_square(far)
    for step_y in range(3):
        if step_y == 1:
            add_cube(far, 1, near)
        add_cube(far, step_y, 1)
    for side in (0, 1):
        forwards[3, side].wait_recv()
    for step_y in (2, 0):
        add_square(near, step_y, far)
        add_cube(near, step_y, far)
    for side in (0, 1):
        forwards[2, side].wait_recv()
    for step_y in (2, 0):
        add_square(far, step_y, near)
        add_cube(far, step_y, near)
    finish_square(1)
    for step_y in range(3):
        for rx in range(3):
            add_cube(1, step_y, rx)
    for index in range(9):
        lanes = pl.ds(128 * (index % 3), 128)
        value = 3.0 * square[index // 3, :, lanes] - 2.0 * (cube[index // 3, :, lanes] * keep(index))
        out_ref[index] = jnp.where(layer == 0, value[:, :64], value[:, 64:])

    for copy in list(z_copies.values()) + row_copies + list(forwards.values()):
        copy.wait_send()


def solution(mesh):
    sizes = dict(mesh.shape)
    rows, cols = sizes["row"], sizes["col"]
    run = min(RUN, cols)

    def whole(*args):
        kernel(rows, cols, run, *args)

    def body(density, retained):
        blocks = density[0, 0].transpose(1, 0, 2).reshape(3, 3, 128, 128)
        kept = retained[0, 0].transpose(0, 2, 1)
        f32, bf16 = jnp.float32, jnp.bfloat16
        dma = pltpu.SemaphoreType.DMA
        result = pl.pallas_call(
            whole,
            out_shape=jax.ShapeDtypeStruct((9, 128, 64), f32),
            in_specs=[pl.BlockSpec(memory_space=pl.ANY), pl.BlockSpec(memory_space=pl.ANY)],
            out_specs=pl.BlockSpec(memory_space=pltpu.VMEM),
            scratch_shapes=[
                pltpu.SMEM((2, 2, 9), jnp.int32),
                pltpu.VMEM((3, 3, 3, 3, 128, 128), f32),
                pltpu.VMEM((3, 3, 3, 128, 384), bf16),
                pltpu.VMEM((3, 3, 3, 128, 384), bf16),
                pltpu.VMEM((3, 3, 256, 128), bf16),
                pltpu.VMEM((3, 3, 256, 128), bf16),
                pltpu.VMEM((3, 128, 384), f32),
                pltpu.VMEM((3, 128, 384), f32),
                dma, dma, dma((3, 2)), dma((3, 2)), dma((2,)), dma((2,)), dma((4, 2)), dma((4, 2)),
            ],
            compiler_params=pltpu.CompilerParams(
                collective_id=0, has_side_effects=True, vmem_limit_bytes=67043328),
        )(blocks, kept)
        return result.transpose(1, 0, 2)[None, None]

    placed = P("row", "col", None, None, None)
    return jax.shard_map(body, mesh=mesh, in_specs=(placed, placed),
                         out_specs=P("row", "col", None, None, "layer"), check_vma=False)
```

time: 39.1 us -> 38.2 us (0.977)
  local copies, waits for them, and re-layouts: 2.68 us -> 2 us
    unnamed x4 -> x0, local copies, waits for them, and re-layouts: 1.74 us -> none
    broadcast_in_dim x1, local copies, waits for them, and re-layouts: 0.93 us -> 2 us  [body(): return result.transpose(1, 0, 2)[None, None]]
where the time goes in v2:
time: 38.2 us; the launch traced here: 37.9 us
  Pallas kernels  35.9 us (94%)
  local copies, waits for them, and re-layouts  2 us (5%)
    pallas_call x1, Pallas kernels, body(): pl.pallas_call(whole, out_shape=jax.ShapeDtypeStruct((9, 128, 64), f32),...  35.9 us
    broadcast_in_dim x1, local copies, waits for them, and re-layouts, body(): return result.transpose(1, 0, 2)[None, None]  2 us

profile of v2, /device:TPU:1, one launch (start us, length us, event | category | flops | bytes accessed | tf_op | source)
XLA Modules:
  0.0 37.9 jit_solution(15171288609700644753)
XLA Ops:
  0.0 35.9 %shard_map.28 = f32[9,128,64]{2,1,0:T(8,128)} custom-call(f32[3,3,128,128]{3,2,1,0:T(8,128)} %bitcast.12, s32[2,2,9]{2,1,0:T(2,128)} %bitcast.13), custom_call_target="tpu_custom_call" | custom-call | tf_op jit(solution)/shard_map/pallas_call | solution.py:212
  35.9 2.0 %copy.3 = f32[1,1,128,9,64]{2,4,3,1,0:T(8,128)} copy(f32[1,1,128,9,64]{4,2,3,1,0:T(8,128)} %bitcast.11) | data formatting | bytes 589824 | tf_op jit(solution)/shard_map/broadcast_in_dim | solution.py:231

commit v3 on v2

--- a/solution.py
+++ b/solution.py
@@ -20,7 +20,7 @@
 
 
 def kernel(rows, cols, run, p_hbm, kept_hbm, out_ref, kept, got, high, low, left, left_cube, square,
-           cube, local_sem, kept_sem, send_z, recv_z, send_row, recv_row, send_fwd, recv_fwd):
+           cube, local_sem, kept_sem, ready, send_z, recv_z, send_row, recv_row, send_fwd, recv_fwd):
     row, col, layer = lax.axis_index("row"), lax.axis_index("col"), lax.axis_index("layer")
     parity = lax.rem(row, 2)
     far, near = 2 * parity, 2 - 2 * parity
@@ -30,46 +30,78 @@
     after = (row, lax.rem(col + 1, cols), lax.rem(layer + lax.div(place + 1, run), 2))
     before = (row, lax.rem(col + cols - 1, cols), lax.rem(layer + lax.div(run - place, run), 2))
 
+    bottom = jnp.logical_and(layer == 0, place == 0)
+
     barrier = pltpu.get_barrier_semaphore()
-    for device in (after, before, far_dev, near_dev):
+    for device in (before, far_dev, near_dev):
         pl.semaphore_signal(barrier, inc=1, device_id=device, device_id_type=MESH)
+
     own = pltpu.make_async_copy(p_hbm, got.at[1, 1], local_sem)
     own.start()
     pattern = pltpu.make_async_copy(kept_hbm, kept, kept_sem)
     pattern.start()
-    pl.semaphore_wait(barrier, 4)
+    pl.semaphore_wait(barrier, 3)
 
     def remote(src, dst, sems, rsems, place, device):
         return pltpu.make_async_remote_copy(
             src_ref=src, dst_ref=dst, send_sem=sems.at[place], recv_sem=rsems.at[place],
             device_id=device, device_id_type=MESH)
 
+    parts = ((1, 0, 2), (far, 0, 1), (far, 1, 1), (near, 0, 1), (near, 1, 1))
     sides = ((before, 2, 0), (after, 0, 1))
-    z_copies = {}
-    for part, which in enumerate((1, far, near)):
-        for side, (device, step, start) in enumerate(sides):
-            z_copies[part, side] = remote(
-                p_hbm.at[which, pl.ds(start, 2)], got.at[1, step, which, pl.ds(start, 2)],
-                send_z, recv_z, (part, side), device)
+
+    def z_copy(part, side, device):
+        which, offset, count = parts[part]
+        step, start = sides[side][1:]
+        ys = pl.ds(start + offset, count)
+        return remote(p_hbm.at[which, ys], got.at[1, step, which, ys], send_z, recv_z,
+                      (part, side), device)
+
+    z_copies = {(part, side): z_copy(part, side, sides[side][0])
+                for part in range(5) for side in (0, 1)}
     row_copies = [
         remote(p_hbm.at[pl.ds(parity, 2)], got.at[near, 1, pl.ds(parity, 2)],
                send_row, recv_row, 0, far_dev),
         remote(p_hbm.at[pl.ds(1 - parity, 2)], got.at[far, 1, pl.ds(1 - parity, 2)],
                send_row, recv_row, 1, near_dev),
     ]
-    z_copies[0, 0].start()
+
     z_copies[0, 1].start()
+    pl.semaphore_signal(ready, inc=1, device_id=after, device_id_type=MESH)
     row_copies[0].start()
     row_copies[1].start()
-    for part in (1, 2):
-        for side in (0, 1):
-            z_copies[part, side].start()
-
-    def forward(slot, which, side, device, place):
+    for part in range(1, 5):
+        z_copies[part, 1].start()
+
+    forwards = {}
+    for side in (0, 1):
         step, start = sides[side][1:]
-        return remote(got.at[1, step, which, pl.ds(start, 2)],
-                      got.at[place, step, which, pl.ds(start, 2)],
-                      send_fwd, recv_fwd, (slot, side), device)
+        for slot, (part, place_x, device) in enumerate((
+                (0, near, far_dev), (0, far, near_dev), (1, near, far_dev), (2, near, far_dev),
+                (3, far, near_dev), (4, far, near_dev))):
+            which, offset, count = parts[part]
+            ys = pl.ds(start + offset, count)
+            forwards[slot, side] = remote(
+                got.at[1, step, which, ys], got.at[place_x, step, which, ys],
+                send_fwd, recv_fwd, (slot, side), device)
+
+    def pass_on(part, side):
+        z_copies[part, side].wait_recv()
+        for slot in ((0, 1), (2,), (3,), (4,), (5,))[part]:
+            forwards[slot, side].start()
+
+    def pass_both(part):
+        pl.when(jnp.logical_not(bottom))(lambda: pass_on(part, 0))
+        pass_on(part, 1)
+
+    @pl.when(bottom)
+    def _():
+        for part in range(5):
+            pass_on(part, 0)
+
+    pl.semaphore_wait(ready, 1)
+    for part in range(5):
+        z_copies[part, 0].start()
 
     def load(step_x, step_y, rx):
         first, count = reach(step_y)
@@ -129,34 +161,22 @@
     add_square(near, 1, 1)
     add_square(near, 1, far)
 
-    forwards = {}
-
-    def send_on(slot, which, side, device, place):
-        copy = forward(slot, which, side, device, place)
-        copy.start()
-        forwards[slot, side] = copy
-
-    for side in (0, 1):
-        z_copies[0, side].wait_recv()
-        send_on(0, 1, side, far_dev, near)
-        send_on(1, 1, side, near_dev, far)
+    pass_both(0)
     for step_y in (2, 0):
         add_square(1, step_y, 1)
     row_copies[0].wait_recv()
     add_square(far, 1, 1)
     add_square(far, 1, near)
-    for side in (0, 1):
-        z_copies[1, side].wait_recv()
-        send_on(2, far, side, far_dev, near)
+    pass_both(1)
+    pass_both(2)
     for step_y in (2, 0):
         add_square(1, step_y, far)
     for side in (0, 1):
         forwards[1, side].wait_recv()
     for step_y in (2, 0):
         add_square(near, step_y, 1)
-    for side in (0, 1):
-        z_copies[2, side].wait_recv()
-        send_on(3, near, side, near_dev, far)
+    pass_both(3)
+    pass_both(4)
     for step_y in (2, 0):
         add_square(1, step_y, near)
     finish_square(near)
@@ -174,12 +194,14 @@
             add_cube(far, 1, near)
         add_cube(far, step_y, 1)
     for side in (0, 1):
-        forwards[3, side].wait_recv()
+        forwards[4, side].wait_recv()
+        forwards[5, side].wait_recv()
     for step_y in (2, 0):
         add_square(near, step_y, far)
         add_cube(near, step_y, far)
     for side in (0, 1):
         forwards[2, side].wait_recv()
+        forwards[3, side].wait_recv()
     for step_y in (2, 0):
         add_square(far, step_y, near)
         add_cube(far, step_y, near)
@@ -190,7 +212,7 @@
     for index in range(9):
         lanes = pl.ds(128 * (index % 3), 128)
         value = 3.0 * square[index // 3, :, lanes] - 2.0 * (cube[index // 3, :, lanes] * keep(index))
-        out_ref[index] = jnp.where(layer == 0, value[:, :64], value[:, 64:])
+        out_ref[index] = jnp.where(layer == 0, value[:, :64], value[:, 64:]).T
 
     for copy in list(z_copies.values()) + row_copies + list(forwards.values()):
         copy.wait_send()
@@ -211,7 +233,7 @@
         dma = pltpu.SemaphoreType.DMA
         result = pl.pallas_call(
             whole,
-            out_shape=jax.ShapeDtypeStruct((9, 128, 64), f32),
+            out_shape=jax.ShapeDtypeStruct((9, 64, 128), f32),
             in_specs=[pl.BlockSpec(memory_space=pl.ANY), pl.BlockSpec(memory_space=pl.ANY)],
             out_specs=pl.BlockSpec(memory_space=pltpu.VMEM),
             scratch_shapes=[
@@ -223,12 +245,13 @@
                 pltpu.VMEM((3, 3, 256, 128), bf16),
                 pltpu.VMEM((3, 128, 384), f32),
                 pltpu.VMEM((3, 128, 384), f32),
-                dma, dma, dma((3, 2)), dma((3, 2)), dma((2,)), dma((2,)), dma((4, 2)), dma((4, 2)),
+                dma, dma, pltpu.SemaphoreType.REGULAR, dma((5, 2)), dma((5, 2)), dma((2,)), dma((2,)),
+                dma((6, 2)), dma((6, 2)),
             ],
             compiler_params=pltpu.CompilerParams(
-                collective_id=0, has_side_effects=True, vmem_limit_bytes=67043328),
-        )(blocks, kept)
-        return result.transpose(1, 0, 2)[None, None]
+                collective_id=0, has_side_effects=True, vmem_limit_bytes=40 << 20),
+        )(*(pltpu.with_memory_space_constraint(x, pltpu.HBM) for x in (blocks, kept)))
+        return result.transpose(2, 0, 1)[None, None]
 
     placed = P("row", "col", None, None, None)
     return jax.shard_map(body, mesh=mesh, in_specs=(placed, placed),

time: 38.2 us -> 35.7 us (0.935)
  local copies, waits for them, and re-layouts: 2 us -> 0.72 us
  Pallas kernels: 35.9 us -> 34.9 us
    broadcast_in_dim x1 -> x0, local copies, waits for them, and re-layouts: 2 us -> none  [body(): return result.transpose(1, 0, 2)[None, None]]
    pallas_call x1, Pallas kernels: 35.9 us -> 34.9 us  [body(): pl.pallas_call(whole, out_shape=jax.ShapeDtypeStruct((9, 64, 128), f32),...]
    unnamed x0 -> x1, local copies, waits for them, and re-layouts: none -> 0.72 us
where the time goes in v3:
time: 35.7 us; the launch traced here: 35.6 us
  Pallas kernels  34.9 us (98%)
  local copies, waits for them, and re-layouts  0.72 us (2%)
    pallas_call x1, Pallas kernels, body(): pl.pallas_call(whole, out_shape=jax.ShapeDtypeStruct((9, 64, 128), f32),...  34.9 us
    unnamed x1, local copies, waits for them, and re-layouts  0.72 us

profile of v3, /device:TPU:1, one launch (start us, length us, event | category | flops | bytes accessed | tf_op | source)
XLA Modules:
  0.0 35.6 jit_solution(16337859585005057598)
XLA Ops:
  0.0 34.9 %shard_map.28 = f32[9,64,128]{2,1,0:T(8,128)S(1)} custom-call(f32[3,3,128,128]{3,2,1,0:T(8,128)} %bitcast.12, s32[2,2,9]{2,1,0:T(2,128)} %bitcast.13), custom_call_target="tpu_custom_call" | custom-call | tf_op jit(solution)/shard_map/pallas_call | solution.py:234
  34.9 0.7 %copy.4 = f32[1,1,128,9,64]{2,4,3,1,0:T(8,128)} copy(f32[1,1,128,9,64]{2,4,3,1,0:T(8,128)S(1)} %bitcast.11) | data formatting | bytes 589824

commit v4 on v3

--- a/solution.py
+++ b/solution.py
@@ -30,7 +30,7 @@
     after = (row, lax.rem(col + 1, cols), lax.rem(layer + lax.div(place + 1, run), 2))
     before = (row, lax.rem(col + cols - 1, cols), lax.rem(layer + lax.div(run - place, run), 2))
 
-    bottom = jnp.logical_and(layer == 0, place == 0)
+    late = jnp.logical_and(layer == 0, jnp.logical_and(col == 0, row < 2))
 
     barrier = pltpu.get_barrier_semaphore()
     for device in (before, far_dev, near_dev):
@@ -66,8 +66,8 @@
                send_row, recv_row, 1, near_dev),
     ]
 
+    pl.semaphore_signal(ready, inc=1, device_id=after, device_id_type=MESH)
     z_copies[0, 1].start()
-    pl.semaphore_signal(ready, inc=1, device_id=after, device_id_type=MESH)
     row_copies[0].start()
     row_copies[1].start()
     for part in range(1, 5):
@@ -89,19 +89,6 @@
         z_copies[part, side].wait_recv()
         for slot in ((0, 1), (2,), (3,), (4,), (5,))[part]:
             forwards[slot, side].start()
-
-    def pass_both(part):
-        pl.when(jnp.logical_not(bottom))(lambda: pass_on(part, 0))
-        pass_on(part, 1)
-
-    @pl.when(bottom)
-    def _():
-        for part in range(5):
-            pass_on(part, 0)
-
-    pl.semaphore_wait(ready, 1)
-    for part in range(5):
-        z_copies[part, 0].start()
 
     def load(step_x, step_y, rx):
         first, count = reach(step_y)
@@ -161,50 +148,55 @@
     add_square(near, 1, 1)
     add_square(near, 1, far)
 
-    pass_both(0)
-    for step_y in (2, 0):
-        add_square(1, step_y, 1)
+    pl.semaphore_wait(ready, 1)
+    for part in range(5):
+        z_copies[part, 0].start()
+
+    @pl.when(late)
+    def _():
+        for part in range(5):
+            pass_on(part, 0)
+            pass_on(part, 1)
+
+    @pl.when(jnp.logical_not(late))
+    def _():
+        for part in range(5):
+            pass_on(part, 0)
+
+    def pass_late(part):
+        pl.when(jnp.logical_not(late))(lambda: pass_on(part, 1))
+
     row_copies[0].wait_recv()
-    add_square(far, 1, 1)
-    add_square(far, 1, near)
-    pass_both(1)
-    pass_both(2)
-    for step_y in (2, 0):
-        add_square(1, step_y, far)
-    for side in (0, 1):
-        forwards[1, side].wait_recv()
-    for step_y in (2, 0):
-        add_square(near, step_y, 1)
-    pass_both(3)
-    pass_both(4)
-    for step_y in (2, 0):
-        add_square(1, step_y, near)
+    for step_x, rx in ((far, 1), (far, near)):
+        add_square(step_x, 1, rx)
+    for rx in range(3):
+        add_square(1, 2, rx)
+    for slot in range(6):
+        forwards[slot, 0].wait_recv()
+    for step_x, rx in ((near, 1), (near, far), (far, 1), (far, near)):
+        add_square(step_x, 2, rx)
+    for part in range(3):
+        pass_late(part)
+    add_square(1, 0, 1)
+    add_square(1, 0, far)
+    forwards[0, 1].wait_recv()
+    add_square(far, 0, 1)
+    finish_square(far)
+    pass_late(3)
+    for step_y, rx in ((0, 1), (1, 1), (2, 1), (1, near), (2, near)):
+        add_cube(far, step_y, rx)
+    pass_late(4)
+    forwards[1, 1].wait_recv()
+    add_square(near, 0, 1)
+    add_square(1, 0, near)
     finish_square(near)
-    for step_y in range(3):
-        if step_y == 1:
-            add_cube(near, 1, far)
-        add_cube(near, step_y, 1)
-    for side in (0, 1):
-        forwards[0, side].wait_recv()
-    for step_y in (2, 0):
-        add_square(far, step_y, 1)
-    finish_square(far)
-    for step_y in range(3):
-        if step_y == 1:
-            add_cube(far, 1, near)
-        add_cube(far, step_y, 1)
-    for side in (0, 1):
-        forwards[4, side].wait_recv()
-        forwards[5, side].wait_recv()
-    for step_y in (2, 0):
-        add_square(near, step_y, far)
-        add_cube(near, step_y, far)
-    for side in (0, 1):
-        forwards[2, side].wait_recv()
-        forwards[3, side].wait_recv()
-    for step_y in (2, 0):
-        add_square(far, step_y, near)
-        add_cube(far, step_y, near)
+    for step_y, rx in ((0, 1), (1, 1), (2, 1), (1, far), (2, far)):
+        add_cube(near, step_y, rx)
+    for slots, step_x, rx in (((2, 3), far, near), ((4, 5), near, far)):
+        for slot in slots:
+            forwards[slot, 1].wait_recv()
+        add_square(step_x, 0, rx)
+        add_cube(step_x, 0, rx)
     finish_square(1)
     for step_y in range(3):
         for rx in range(3):

time: 35.7 us -> 38.4 us (1.076)
  Pallas kernels: 34.9 us -> 37.5 us
    pallas_call x1, Pallas kernels: 34.9 us -> 37.5 us  [body(): pl.pallas_call(whole, out_shape=jax.ShapeDtypeStruct((9, 64, 128), f32),...]
where the time goes in v4:
time: 38.4 us; the launch traced here: 38.2 us
  Pallas kernels  37.5 us (98%)
  local copies, waits for them, and re-layouts  0.72 us (2%)
    pallas_call x1, Pallas kernels, body(): pl.pallas_call(whole, out_shape=jax.ShapeDtypeStruct((9, 64, 128), f32),...  37.5 us

profile of v4, /device:TPU:1, one launch (start us, length us, event | category | flops | bytes accessed | tf_op | source)
XLA Modules:
  0.0 38.2 jit_solution(11751906926310881815)
XLA Ops:
  0.0 37.5 %shard_map.28 = f32[9,64,128]{2,1,0:T(8,128)S(1)} custom-call(f32[3,3,128,128]{3,2,1,0:T(8,128)} %bitcast.12, s32[2,2,9]{2,1,0:T(2,128)} %bitcast.13), custom_call_target="tpu_custom_call" | custom-call | tf_op jit(solution)/shard_map/pallas_call | solution.py:226
  37.5 0.7 %copy.4 = f32[1,1,128,9,64]{2,4,3,1,0:T(8,128)} copy(f32[1,1,128,9,64]{2,4,3,1,0:T(8,128)S(1)} %bitcast.11) | data formatting | bytes 589824

commit v5 on v3

--- a/solution.py
+++ b/solution.py
@@ -30,7 +30,7 @@
     after = (row, lax.rem(col + 1, cols), lax.rem(layer + lax.div(place + 1, run), 2))
     before = (row, lax.rem(col + cols - 1, cols), lax.rem(layer + lax.div(run - place, run), 2))
 
-    bottom = jnp.logical_and(layer == 0, place == 0)
+    bottom = jnp.logical_and(jnp.logical_and(layer == 0, place == 0), row + col > 1)
 
     barrier = pltpu.get_barrier_semaphore()
     for device in (before, far_dev, near_dev):
@@ -66,8 +66,8 @@
                send_row, recv_row, 1, near_dev),
     ]
 
+    pl.semaphore_signal(ready, inc=1, device_id=after, device_id_type=MESH)
     z_copies[0, 1].start()
-    pl.semaphore_signal(ready, inc=1, device_id=after, device_id_type=MESH)
     row_copies[0].start()
     row_copies[1].start()
     for part in range(1, 5):
@@ -94,14 +94,14 @@
         pl.when(jnp.logical_not(bottom))(lambda: pass_on(part, 0))
         pass_on(part, 1)
 
+    pl.semaphore_wait(ready, 1)
+    for part in range(5):
+        z_copies[part, 0].start()
+
     @pl.when(bottom)
     def _():
         for part in range(5):
             pass_on(part, 0)
-
-    pl.semaphore_wait(ready, 1)
-    for part in range(5):
-        z_copies[part, 0].start()
 
     def load(step_x, step_y, rx):
         first, count = reach(step_y)

time: 35.7 us -> 35.7 us (level)
  no operation moved by 1% of the time
where the time goes in v5:
time: 35.7 us; the launch traced here: 35.6 us
  Pallas kernels  34.9 us (98%)
  local copies, waits for them, and re-layouts  0.72 us (2%)
    pallas_call x1, Pallas kernels, body(): pl.pallas_call(whole, out_shape=jax.ShapeDtypeStruct((9, 64, 128), f32),...  34.9 us
    unnamed x1, local copies, waits for them, and re-layouts  0.72 us

profile of v5, /device:TPU:1, one launch (start us, length us, event | category | flops | bytes accessed | tf_op | source)
XLA Modules:
  0.0 35.6 jit_solution(142573903959384782)
XLA Ops:
  0.0 34.9 %shard_map.28 = f32[9,64,128]{2,1,0:T(8,128)S(1)} custom-call(f32[3,3,128,128]{3,2,1,0:T(8,128)} %bitcast.12, s32[2,2,9]{2,1,0:T(2,128)} %bitcast.13), custom_call_target="tpu_custom_call" | custom-call | tf_op jit(solution)/shard_map/pallas_call | solution.py:234
  34.9 0.7 %copy.4 = f32[1,1,128,9,64]{2,4,3,1,0:T(8,128)} copy(f32[1,1,128,9,64]{2,4,3,1,0:T(8,128)S(1)} %bitcast.11) | data formatting | bytes 589824
